TPU v7x, 256 devices: a whole 4x4x8 slice. The times are simulated.
256 devices in a mesh: src: 16 (over y, z_lo), snk: 16 (over x, z_hi, core).
Axes of the slice: x: 4, y: 4, z: 8 (z_hi: 2, z_lo: 4; z = z_hi * 4 + z_lo), core: 2. Of those that a mesh axis runs over, the one named last changes fastest.
Arguments:
- perambulator: bfloat16 [16, 16, 2, 512, 512], P('src', 'snk'), may hold values from -0.375 to 0.375
- meson_field: bfloat16 [16, 27, 2, 128, 128], P('snk', None, None, 'src'), may hold values from -0.5 to 0.5
- op_momentum: int32 [4], replicated, may hold values from 0 to 26
- op_gamma: int32 [4], replicated, may hold values from 0 to 15
Outputs:
- loops: float32 [512, 16, 4, 2, 512], P('snk', 'src')
Inputs may be any that keep to these rules, and one draw needn't show every extreme that they name: `op_momentum`: index into the momenta of the meson-field table. `op_gamma`: index n of Gamma_n.
All inputs are finite; a program needn't handle non-finite values.
Results may differ from a plain program's by a relative error of at most 0.0029.
Values may be sent and summed in bfloat16 or wider, within the bound.
A program may use at most 64 MiB of HBM per device.

v0:
```python
import jax
import jax.numpy as jnp
import numpy as np
from jax import lax
from jax.sharding import Mesh
from jax.sharding import PartitionSpec as P

SNK = ("snk_0", "snk_1", "snk_2")


def copy_for_each(value, axis):
    copies = jnp.broadcast_to(value, (lax.axis_size(axis), *value.shape))
    return lax.all_to_all(copies, axis, split_axis=0, concat_axis=0, tiled=True)


def in_order(parts, dim):
    dims = list(parts.shape[1:])
    dims[dim] *= parts.shape[0]
    return jnp.moveaxis(parts, 0, dim).reshape(dims)


def collect(value, axis, dim):
    parts = copy_for_each(value, axis)
    return in_order(parts, dim)


def split_up(value, dim, size):
    before, after = (value.shape[:dim], value.shape[dim + 1 :])
    return jnp.moveaxis(value.reshape(*before, size, -1, *after), dim, 0)


def summed_rows(value, chips, core, dim):
    sizes = (lax.axis_size(chips), lax.axis_size(core))
    parts = split_up(value, dim, sizes[0] * sizes[1])
    inside = parts.shape[1:]
    parts = parts.reshape(*sizes, *inside).swapaxes(0, 1).reshape(-1, *inside)
    parts = lax.psum_scatter(parts, core, scatter_dimension=0, tiled=True)
    return lax.psum_scatter(parts, chips, scatter_dimension=0, tiled=True)[0]


def gamma_table():
    zero_block = np.zeros((4, 4))
    basis_list = [
        (
            zero_block,
            np.array([[0, 0, 0, 1], [0, 0, 1, 0], [0, -1, 0, 0], [-1, 0, 0, 0]], dtype=float),
        ),
        (
            np.array([[0, 0, 0, -1], [0, 0, 1, 0], [0, 1, 0, 0], [-1, 0, 0, 0]], dtype=float),
            zero_block,
        ),
        (
            zero_block,
            np.array([[0, 0, 1, 0], [0, 0, 0, -1], [-1, 0, 0, 0], [0, 1, 0, 0]], dtype=float),
        ),
        (
            np.array([[0, 0, 1, 0], [0, 0, 0, 1], [1, 0, 0, 0], [0, 1, 0, 0]], dtype=float),
            zero_block,
        ),
    ]
    real_list = []
    imag_list = []
    for number in range(16):
        mat_re = np.eye(4)
        mat_im = np.zeros((4, 4))
        for bit_index in range(4):
            if number >> bit_index & 1:
                other_re, other_im = basis_list[bit_index]
                mat_re, mat_im = (
                    mat_re @ other_re - mat_im @ other_im,
                    mat_re @ other_im + mat_im @ other_re,
                )
        real_list.append(mat_re)
        imag_list.append(mat_im)
    return (np.stack(real_list), np.stack(imag_list))


def on_device(perambulator, meson_field, op_momentum, op_gamma):
    src_devices = lax.axis_size("src")
    snk_devices = lax.axis_size(SNK)
    group_size = src_devices // snk_devices
    sources = perambulator.shape[0]
    sink_count = perambulator.shape[1]
    spin_modes = perambulator.shape[3]
    momenta_count = meson_field.shape[1]
    mode_count = meson_field.shape[4]
    spin_count = spin_modes // mode_count
    operators = op_gamma.shape[0]
    gamma_re, gamma_im = gamma_table()
    spin_sign = gamma_re[15][[0, 1, 2, 3], [0, 1, 2, 3]]
    column_sign = jnp.asarray(np.repeat(spin_sign, mode_count), jnp.bfloat16)
    table_re = jnp.asarray((gamma_re * spin_sign[None, None, :]).reshape(16, 16), jnp.float32)
    table_im = jnp.asarray((gamma_im * spin_sign[None, None, :]).reshape(16, 16), jnp.float32)
    pick_gamma = (op_gamma[:, None] == jnp.arange(16, dtype=jnp.int32)[None, :]).astype(jnp.float32)
    chosen_re = jnp.dot(pick_gamma, table_re, precision=lax.Precision.HIGHEST).reshape(
        operators, spin_count, spin_count
    )
    chosen_im = jnp.dot(pick_gamma, table_im, precision=lax.Precision.HIGHEST).reshape(
        operators, spin_count, spin_count
    )
    gamma_pair = jnp.stack(
        [jnp.stack([chosen_re, chosen_im], axis=2), jnp.stack([-chosen_im, chosen_re], axis=2)],
        axis=1,
    ).astype(jnp.bfloat16)
    pick_momentum = (
        op_momentum[:, None] == jnp.arange(momenta_count, dtype=jnp.int32)[None, :]
    ).astype(jnp.bfloat16)
    selected = jnp.einsum(
        "kp,bpimn->bkimn", pick_momentum, meson_field, preferred_element_type=jnp.float32
    ).astype(jnp.bfloat16)
    fields = collect(selected, "src", 3)
    forward = perambulator.reshape(sources, sink_count, 2, spin_modes, spin_count, mode_count)
    turned = jnp.einsum(
        "abirsm,kisjt->bkratjm", forward, gamma_pair, preferred_element_type=jnp.float32
    ).astype(jnp.bfloat16)
    turned = turned.reshape(sink_count, operators, spin_modes, sources, spin_count, 2 * mode_count)
    top_half = jnp.concatenate([fields[:, :, 0], fields[:, :, 1]], axis=-1)
    low_half = jnp.concatenate([-fields[:, :, 1], fields[:, :, 0]], axis=-1)
    mixing = jnp.concatenate([top_half, low_half], axis=-2)
    front = jnp.einsum(
        "bkratx,bkxy->bkraty", turned, mixing, preferred_element_type=jnp.float32
    ).astype(jnp.bfloat16)
    front = front.reshape(group_size, sources, operators, spin_modes, sources, 2 * spin_modes)
    piece_rows = spin_modes // snk_devices
    pieces = perambulator.reshape(sources, sink_count, 2, snk_devices, piece_rows, spin_modes)
    by_sink = lax.all_to_all(pieces, SNK, split_axis=3, concat_axis=1, tiled=True)
    by_owner = lax.all_to_all(by_sink, "src", split_axis=1, concat_axis=0, tiled=True)
    joined = lax.all_to_all(by_owner, SNK, split_axis=0, concat_axis=3, tiled=True)
    joined = joined.reshape(group_size, sources, sources, 2, spin_modes, spin_modes)
    blocks = jnp.transpose(joined, (1, 0, 2, 3, 4, 5))
    mirror_re = blocks[:, :, :, 0].reshape(
        sources, group_size, sources, spin_modes, spin_count, mode_count
    )
    mirror_im = blocks[:, :, :, 1].reshape(
        sources, group_size, sources, spin_modes, spin_count, mode_count
    )
    real_row = jnp.stack([mirror_re, mirror_im], axis=5)
    imag_row = jnp.stack([-mirror_im, mirror_re], axis=5)
    weights = jnp.stack([real_row, imag_row], axis=3).reshape(
        sources, group_size, sources, 2, spin_modes, 2 * spin_modes
    )
    weights = weights * column_sign[:, None]
    return summed_rows(
        jnp.einsum("uvkraq,vuapcq->rakpc", front, weights, preferred_element_type=jnp.float32),
        ("snk_0", "snk_1"),
        "snk_2",
        0,
    )


def solution(mesh):
    finer = Mesh(
        mesh.devices.reshape(mesh.shape["src"], 4, 2, 2), ("src", "snk_0", "snk_1", "snk_2")
    )
    return jax.shard_map(
        on_device,
        mesh=finer,
        in_specs=(P("src", SNK, None, None, None), P(SNK, None, None, "src", None), P(), P()),
        out_specs=P(SNK, "src", None, None, None),
        check_vma=False,
    )
```

profile of v0, /device:TPU:1, one launch (start us, length us, event | category | flops | bytes accessed | tf_op | source)
XLA Modules:
  0.0 297.2 jit_solution(12854834074866878969)
XLA Ops:
  6.5 0.9 copy-done
  7.4 0.9 convolution_convert_fusion.1
  8.3 0.8 broadcast_in_dim.2
  9.1 9.2 %all-to-all-start.3 = ((bf16[16,1,4,2,8,128]{5,4,3,2,1,0:T(8,128)(2,1)}), bf16[16,1,4,2,8,128]{5,4,3,2,1,0:T(8,128)(2,1)S(1)}, u32[]{:S(2)}, u32[]{:S(2)}) async-start(bf16[16,1,4,2,8,128]{5,4,3,2,1,0:T(8,128)(2,1)} %broadcast_in_dim.2), calls=%async_computation.3 | async-start | bytes 524288 | tf_op jit(solution)/shard_map/all_to_all | solution.py:13
  18.2 1.3 copy.72
  19.6 8.6 %all-to-all-done.3 = bf16[16,1,4,2,8,128]{5,4,3,2,1,0:T(8,128)(2,1)S(1)} async-done(((bf16[16,1,4,2,8,128]{5,4,3,2,1,0:T(8,128)(2,1)}), bf16[16,1,4,2,8,128]{5,4,3,2,1,0:T(8,128)(2,1)S(1)}, u32[]{:S(2)}, u32[]{:S(2)}) %all-to-all-start.3) | async-done | bytes 262176 | tf_op jit(solution)/shard_map/all_to_all | solution.py:13
  28.2 35.8 %all_to_all.50 = bf16[1,1,2,16,32,512]{5,4,2,1,0,3:T(8,128)(2,1)} all-to-all(bf16[1,1,2,16,32,512]{5,4,2,1,0,3:T(8,128)(2,1)S(1)} %copy.72), channel_id=1, replica_groups=mesh['src'=16,'snk_0'=4,'snk_1'=2,'snk_2'=2] {'snk_0','snk_1','snk_2'}, dimensions={3} | all-to-all | bytes 2097152 | tf_op jit(solution)/shard_map/all_to_all | solution.py:126
  63.9 7.2 %all-to-all-start.1 = ((bf16[1,16,2,1,32,512]{5,4,2,3,0,1:T(8,128)(2,1)}), bf16[1,16,2,1,32,512]{5,4,2,3,0,1:T(8,128)(2,1)}, u32[]{:S(2)}, u32[]{:S(2)}) async-start(bf16[1,16,2,1,32,512]{5,4,2,3,0,1:T(8,128)(2,1)} %bitcast.4), calls=%async_computation.1 | async-start | bytes 2097152 | tf_op jit(solution)/shard_map/all_to_all | solution.py:127
  71.1 0.3 reshape.101
  71.4 26.8 %all-to-all-done.1 = bf16[1,16,2,1,32,512]{5,4,2,3,0,1:T(8,128)(2,1)} async-done(((bf16[1,16,2,1,32,512]{5,4,2,3,0,1:T(8,128)(2,1)}), bf16[1,16,2,1,32,512]{5,4,2,3,0,1:T(8,128)(2,1)}, u32[]{:S(2)}, u32[]{:S(2)}) %all-to-all-start.1) | async-done | bytes 1048608 | tf_op jit(solution)/shard_map/all_to_all | solution.py:127
  98.2 5.1 %all-to-all-start.2 = ((bf16[16,1,2,1,32,512]{5,4,2,3,1,0:T(8,128)(2,1)}), bf16[16,1,2,1,32,512]{5,4,2,3,1,0:T(8,128)(2,1)S(1)}, u32[]{:S(2)}, u32[]{:S(2)}) async-start(bf16[16,1,2,1,32,512]{5,4,2,3,1,0:T(8,128)(2,1)} %bitcast.6), calls=%async_computation.2 | async-start | bytes 2097152 | tf_op jit(solution)/shard_map/all_to_all | solution.py:128
  103.6 0.2 convolution_convert_fusion.2
  104.3 4.7 %fusion = bf16[1,4,512,1,4,2,128]{6,4,2,5,1,0,3:T(4,128)(2,1)} fusion(bf16[2,512,4,128]{3,2,1,0:T(4,128)(2,1)S(1)} %reshape.101, bf16[4,1,4,2,4]{2,4,1,3,0:T(4,128)(2,1)S(1)} %copy.83, bf16[4,1,4,2,4]{2,4,1,3,0:T(4,128)(2,1)S(1)} %copy.82), kind=kOutput, calls=%fused_computation.1 | convolution fusion | flops 35652608 | bytes 5243392 | tf_op jit(solution)/shard_map/abirsm,kisjt->bkratjm/dot_general | solution.py:113
  109.0 7.5 %copy.85 = bf16[1,4,512,1,4,2,128]{2,6,5,4,1,3,0:T(8,128)(2,1)} copy(bf16[1,4,512,1,4,2,128]{6,4,2,5,1,0,3:T(4,128)(2,1)} %fusion) | data formatting | bytes 8388608 | tf_op jit(solution)/shard_map/convert_element_type | solution.py:115
  116.9 5.4 %convolution_convert_fusion = bf16[4,512,4,256]{1,3,2,0:T(8,128)(2,1)} fusion(bf16[4,512,4,256]{1,3,2,0:T(8,128)(2,1)} %bitcast.91, bf16[1,4,128,128]{2,3,1,0:T(8,128)(2,1)S(1)} %bitcast.103, bf16[1,4,128,128]{2,3,1,0:T(8,128)(2,1)S(1)} %bitcast_negate_fusion, bf16[1,4,128,128]{2,3,1,0:T(8,128)(2,1)S(1)} %bitcast.99), kind=kOutput, calls=%fused_computation.2 | convolution fusion | flops 1077936128 | bytes 8781824 | tf_op jit(solution)/shard_map/bkratx,bkxy->bkraty/dot_general | solution.py:120
  122.3 7.6 %all-to-all-done.2 = bf16[16,1,2,1,32,512]{5,4,2,3,1,0:T(8,128)(2,1)S(1)} async-done(((bf16[16,1,2,1,32,512]{5,4,2,3,1,0:T(8,128)(2,1)}), bf16[16,1,2,1,32,512]{5,4,2,3,1,0:T(8,128)(2,1)S(1)}, u32[]{:S(2)}, u32[]{:S(2)}) %all-to-all-start.2) | async-done | bytes 1048608 | tf_op jit(solution)/shard_map/all_to_all | solution.py:128
  130.2 0.2 copy.77
  130.5 0.2 copy.76
  131.1 1.8 copy-done.1
  132.9 4.8 %fusion.2 = f32[2,512,4,512]{1,3,2,0:T(8,128)S(1)} fusion(bf16[4,512,1024,1]{1,2,0,3:T(8,128)(2,1)S(1)} %bitcast.95, bf16[1,512,1024]{1,2,0:T(8,128)(2,1)S(1)} %bitcast.101, bf16[1,512,1024]{1,2,0:T(8,128)(2,1)S(1)} %bitcast.100, bf16[512]{0:T(512)(128)(2,1)S(1)} %copy-done.6), kind=kOutput, calls=%fused_computation.5 | convolution fusion | flops 4301258752 | bytes 14681088 | tf_op jit(solution)/shard_map/uvkraq,vuapcq->rakpc/dot_general | solution.py:144
  137.7 4.3 %copy.94 = f32[2,8,32,1,4,2,512]{6,2,5,4,1,0,3:T(8,128)} copy(f32[2,8,32,1,4,2,512]{6,2,0,1,4,5,3:T(8,128)S(1)} %bitcast.92) | data formatting | bytes 16777216 | tf_op jit(solution)/shard_map/transpose | solution.py:36
  142.1 18.9 %reduce-scatter.3.cloned.1.call-done = f32[8,32,1,4,2,512]{5,1,4,3,2,0:T(8,128)} async-done(((f32[16,32,1,4,2,512]{5,1,4,3,2,0:T(8,128)}), f32[8,32,1,4,2,512]{5,1,4,3,2,0:T(8,128)}) %reduce-scatter.3.cloned.1.call-update) | async-done | bytes 4194320 | tf_op jit(solution)/shard_map/reduce_scatter | solution.py:37
  161.1 127.1 %reduce-scatter.5.cloned.1.call-done = f32[1,32,1,4,2,512]{5,1,4,3,2,0:T(8,128)} async-done(((f32[8,32,1,4,2,512]{5,1,4,3,2,0:T(8,128)}), f32[1,32,1,4,2,512]{5,1,4,3,2,0:T(8,128)}) %reduce-scatter.5.cloned.1.call-update) | async-done | bytes 524304 | tf_op jit(solution)/shard_map/reduce_scatter | solution.py:38
  288.2 2.2 copy.95
  (35 shorter events, 1.9 us)
Async XLA Ops:
  6.5 0.9 copy-start
  6.5 64.5 %copy-start.2 = (bf16[1,1,2,512,512]{4,3,2,1,0:T(8,128)(2,1)S(1)}, bf16[1,1,2,512,512]{4,3,2,1,0:T(8,128)(2,1)}, u32[]{:S(2)}) copy-start(bf16[1,1,2,512,512]{4,3,2,1,0:T(8,128)(2,1)} %param.7) | copy-start | bytes 3145732
  9.1 19.1 %all-to-all-start.3 = ((bf16[16,1,4,2,8,128]{5,4,3,2,1,0:T(8,128)(2,1)}), bf16[16,1,4,2,8,128]{5,4,3,2,1,0:T(8,128)(2,1)S(1)}, u32[]{:S(2)}, u32[]{:S(2)}) async-start(bf16[16,1,4,2,8,128]{5,4,3,2,1,0:T(8,128)(2,1)} %broadcast_in_dim.2), calls=%async_computation.3 | async-start | bytes 524288 | tf_op jit(solution)/shard_map/all_to_all | solution.py:13
  19.5 83.8 %copy-start.3 = (s32[4]{0:T(128)S(1)}, s32[4]{0:T(128)}, u32[]{:S(2)}) copy-start(s32[4]{0:T(128)} %param.10) | copy-start | bytes 52
  19.6 83.8 %copy-start.4 = (f32[16,16]{1,0:T(8,128)S(1)}, f32[16,16]{1,0:T(8,128)}, u32[]{:S(2)}) copy-start(f32[16,16]{1,0:T(8,128)} %constant.8.clone) | copy-start | bytes 3076
  19.6 84.1 %copy-start.5 = (f32[16,16]{1,0:T(8,128)S(1)}, f32[16,16]{1,0:T(8,128)}, u32[]{:S(2)}) copy-start(f32[16,16]{1,0:T(8,128)} %constant.7.clone) | copy-start | bytes 3076
  63.9 34.3 %all-to-all-start.1 = ((bf16[1,16,2,1,32,512]{5,4,2,3,0,1:T(8,128)(2,1)}), bf16[1,16,2,1,32,512]{5,4,2,3,0,1:T(8,128)(2,1)}, u32[]{:S(2)}, u32[]{:S(2)}) async-start(bf16[1,16,2,1,32,512]{5,4,2,3,0,1:T(8,128)(2,1)} %bitcast.4), calls=%async_computation.1 | async-start | bytes 2097152 | tf_op jit(solution)/shard_map/all_to_all | solution.py:127
  98.2 31.8 %all-to-all-start.2 = ((bf16[16,1,2,1,32,512]{5,4,2,3,1,0:T(8,128)(2,1)}), bf16[16,1,2,1,32,512]{5,4,2,3,1,0:T(8,128)(2,1)S(1)}, u32[]{:S(2)}, u32[]{:S(2)}) async-start(bf16[16,1,2,1,32,512]{5,4,2,3,1,0:T(8,128)(2,1)} %bitcast.6), calls=%async_computation.2 | async-start | bytes 2097152 | tf_op jit(solution)/shard_map/all_to_all | solution.py:128
  103.3 57.8 %reduce-scatter.3.cloned.1.call-start = ((), (), s32[]{:S(2)}) async-start(), calls=%async_computation.6 | async-start | bytes 12582912 | tf_op jit(solution)/shard_map/reduce_scatter | solution.py:37
  130.7 2.2 copy-start.1
  130.7 2.2 copy-start.6
  142.1 146.1 %reduce-scatter.5.cloned.1.call-start = ((), (), s32[]{:S(2)}) async-start(), calls=%async_computation.7 | async-start | bytes 4718592 | tf_op jit(solution)/shard_map/reduce_scatter | solution.py:38
Sparse Core Ops, SparseCore 0:
  142.2 18.8 reduce-scatter.2
  165.2 122.9 reduce-scatter.4
where the time goes:
time: 299 us; the launch traced here: 297 us
  waiting for transfers between devices  189 us (63%)
  blocking collectives  35.8 us (12%)
  starting transfers between devices  21.5 us (7%)
  local copies, waits for them, and re-layouts  20.8 us (7%)
  matrix products  16.2 us (5%)
  between operations  13.6 us (5%)
    reduce_scatter x1, waiting for transfers between devices, summed_rows(): return lax.psum_scatter(parts, chips, scatter_dimension=0, tiled=True)[0]  127 us
    all_to_all x1, blocking collectives, on_device(): lax.all_to_all(pieces, SNK, split_axis=3, concat_axis=1, tiled=True)  35.8 us
    all_to_all x1, waiting for transfers between devices, on_device(): lax.all_to_all(by_sink, 'src', split_axis=1, concat_axis=0, tiled=True)  26.8 us
    reduce_scatter x1, waiting for transfers between devices, summed_rows(): parts = lax.psum_scatter(parts, core, scatter_dimension=0, tiled=True)  18.9 us
    all_to_all x1, starting transfers between devices, copy_for_each(): return lax.all_to_all(copies, axis, split_axis=0, concat_axis=0, tiled=True)  9.17 us
    all_to_all x1, waiting for transfers between devices, copy_for_each(): return lax.all_to_all(copies, axis, split_axis=0, concat_axis=0, tiled=True)  8.58 us
    all_to_all x1, waiting for transfers between devices, on_device(): lax.all_to_all(by_owner, SNK, split_axis=0, concat_axis=3, tiled=True)  7.64 us
    convert_element_type x1, local copies, waits for them, and re-layouts, on_device(): turned = jnp.einsum('abirsm,kisjt->bkratjm', forward, gamma_pair, preferr...  7.49 us
  transfers between devices with their start and end apart: 5, of which 5 were waited for; matrix products, arithmetic and copies ran while one was open for 7% of the time, Pallas kernels for 0%

commit v1 on v0

v1 whole, which is shorter than its diff:
```python
import jax
import jax.numpy as jnp
import numpy as np
from jax import lax
from jax.experimental import pallas as pl
from jax.experimental.pallas import tpu as pltpu
from jax.sharding import PartitionSpec as P

MESH = pl.DeviceIdType.MESH
NX, NY, NZ = 4, 4, 8
CHUNKS = 4
BF, F32 = jnp.bfloat16, jnp.float32


def gamma_table():
    zero = np.zeros((4, 4))
    basis = [
        (zero, np.array([[0, 0, 0, 1], [0, 0, 1, 0], [0, -1, 0, 0], [-1, 0, 0, 0]], dtype=float)),
        (np.array([[0, 0, 0, -1], [0, 0, 1, 0], [0, 1, 0, 0], [-1, 0, 0, 0]], dtype=float), zero),
        (zero, np.array([[0, 0, 1, 0], [0, 0, 0, -1], [-1, 0, 0, 0], [0, 1, 0, 0]], dtype=float)),
        (np.array([[0, 0, 1, 0], [0, 0, 0, 1], [1, 0, 0, 0], [0, 1, 0, 0]], dtype=float), zero),
    ]
    table = []
    for number in range(16):
        mat = np.eye(4, dtype=complex)
        for bit in range(4):
            if number >> bit & 1:
                mat = mat @ (basis[bit][0] + 1j * basis[bit][1])
        table.append(mat)
    return np.stack(table)


def spin_table():
    table = gamma_table()
    g5 = np.real(np.diagonal(table[15]))
    rows = np.argmax(np.abs(table), axis=1)
    entry = np.take_along_axis(table, rows[:, None, :], axis=1)[:, 0, :] * g5[None, :]
    flat = np.stack([rows, np.real(entry), np.imag(entry)]).round().astype(np.int32)
    return flat.reshape(3 * 64)


def place(x, y, z, c):
    return (y * 4 + z % 4, x * 4 + (z // 4) * 2 + c)


def kernel(gam, mom, tab, tau, mes, out, field, field_b, half, half_b, mir, front, turn, mine, xs, xr, keep, zs, zr,
           s_loc, s_half, r_half, s_f1, r_f1, s_f2, r_f2, s_f3, r_f3, s_mir, r_mir, s_fwd, r_fwd,
           s_x, r_x, s_z, r_z):
    src, snk = lax.axis_index("src"), lax.axis_index("snk")
    x, y, zh, zl, c = snk // 4, src // 4, (snk // 2) % 2, src % 4, snk % 2
    z = zh * 4 + zl
    l1, l0 = zl // 2, zl % 2
    other = 1 - c
    partner = place(x, y, z, other)
    mirror = place(y, x, l1 * 4 + zh * 2 + c, l0)
    own_mirror = (mirror[0] == src) & (mirror[1] == snk)
    far_mirror = jnp.logical_not(own_mirror)
    zl_peers = [place(x, y, zh * 4 + (zl + d) % 4, c) for d in (1, 2, 3)]
    y_peers = [place(x, (y + d) % 4, z, c) for d in (1, 2, 3)]
    x_peers = [place((x + d) % 4, y, z, c) for d in (1, 2, 3)]
    z_peer = place(x, y, (z + 4) % 8, c)

    bar = pltpu.get_barrier_semaphore()
    for dev in [partner, z_peer, *zl_peers, *y_peers, *x_peers]:
        pl.semaphore_signal(bar, inc=1, device_id=dev, device_id_type=MESH)

    @pl.when(far_mirror)
    def _():
        pl.semaphore_signal(bar, inc=1, device_id=mirror, device_id_type=MESH)

    for k in range(4):
        field[k, :, src] = mes[0, mom[k]]
    local = [
        pltpu.make_async_copy(
            tau.at[p, :, c, :, s * 128 : (s + 1) * 128], half.at[p, s], s_loc.at[p, s]
        )
        for p in range(2)
        for s in range(4)
    ]
    for cp in local:
        cp.start()

    pl.semaphore_wait(bar, jnp.where(far_mirror, 12, 11))

    def send(a, b, ss, rs, dev):
        return pltpu.make_async_remote_copy(
            src_ref=a, dst_ref=b, send_sem=ss, recv_sem=rs, device_id=dev, device_id_type=MESH
        )

    f1 = [
        send(field.at[:, :, src], field.at[:, :, src], s_f1.at[d], r_f1.at[d], zl_peers[d])
        for d in range(3)
    ]
    for cp in f1:
        cp.start()
    swap = [
        send(
            tau.at[p, :, other, :, s * 128 : (s + 1) * 128],
            half_b.at[p, s],
            s_half.at[p, s],
            r_half.at[p, s],
            partner,
        )
        for p in range(2)
        for s in range(4)
    ]
    for cp in swap:
        cp.start()
    mcopy = [
        send(tau.at[:, pl.ds(2 * j, 2)], mir.at[0, j], s_mir.at[j], r_mir.at[j], mirror)
        for j in range(CHUNKS)
    ]
    mlocal = [
        pltpu.make_async_copy(tau.at[:, pl.ds(2 * j, 2)], mir.at[0, j], r_mir.at[j])
        for j in range(CHUNKS)
    ]

    @pl.when(far_mirror)
    def _():
        for cp in mcopy:
            cp.start()

    @pl.when(own_mirror)
    def _():
        for cp in mlocal:
            cp.start()

    for d in range(3):
        send(field.at[:, :, src], field.at[:, :, src], s_f1.at[d], r_f1.at[d], zl_peers[d]).wait_recv()
    rows = field.at[:, :, pl.ds(4 * y, 4)]
    f2 = [send(rows, rows, s_f2.at[d], r_f2.at[d], y_peers[d]) for d in range(3)]
    for cp in f2:
        cp.start()
    for cp in f2:
        cp.wait_recv()
    f3 = send(field, field_b, s_f3, r_f3, partner)
    f3.start()
    for cp in local:
        cp.wait()

    def make_front(b, field, half):
        def for_op(k, carry):
            gamma = gam[k]
            m_re = field[k, 0].astype(F32).reshape(128, 128)
            m_im = field[k, 1].astype(F32).reshape(128, 128)
            for t in range(4):
                spin = tab[gamma * 4 + t]
                g_re = tab[64 + gamma * 4 + t].astype(F32)
                g_im = tab[128 + gamma * 4 + t].astype(F32)
                top = (g_re * m_re - g_im * m_im).astype(BF)
                low = (g_re * m_im + g_im * m_re).astype(BF)
                mix = jnp.concatenate(
                    [jnp.concatenate([top, low], axis=1), jnp.concatenate([-low, top], axis=1)], axis=0
                )
                left = jnp.concatenate(
                    [half[0, spin].reshape(256, 128), half[1, spin].reshape(256, 128)], axis=1
                )
                made = jnp.dot(left, mix, preferred_element_type=F32).astype(BF)
                made = made.reshape(4, 2, 32, 256)
                front[b, 0, :, :, k, :, t * 128 : (t + 1) * 128] = made[..., :128]
                front[b, 1, :, :, k, :, t * 128 : (t + 1) * 128] = made[..., 128:]
            return carry

        lax.fori_loop(0, 4, for_op, 0)

    make_front(0, field, half)
    f3.wait_recv()
    for cp in swap:
        cp.wait_recv()
    make_front(1, field_b, half_b)

    def x_copy(j, d):
        return send(xs.at[j, d], xr.at[j, d], s_x.at[j, d], r_x.at[j, d], x_peers[d])

    def z_copy(j):
        return send(zs.at[j], zr.at[j], s_z.at[j], r_z.at[j], z_peer)

    def product(j):
        for b in (0, 1):
            re = mir[b, j, 0].reshape(128, 512)
            im = mir[b, j, 1].reshape(128, 512)
            if j >= 2:
                re, im = -re, -im
            turn[b, 0] = jnp.concatenate([re, -im], axis=0).T
            turn[b, 1] = jnp.concatenate([im, re], axis=0).T

        def part(row):
            total = jnp.zeros((256, 256), F32)
            for b in (0, 1):
                for p in (0, 1):
                    total += jnp.dot(
                        front[b, p, row].reshape(256, 512), turn[b, p], preferred_element_type=F32
                    )
            return total

        for d in (1, 0, 2):
            xs[j, d] = part((x + d + 1) % 4).astype(BF)
            x_copy(j, d).start()
        mine[j] = part(x)

    def over_x(j):
        for d in range(3):
            x_copy(j, d).wait_recv()

        def rows_of(which):
            at = pl.ds(pl.multiple_of(which * 128, 128), 128)
            total = mine[j, at]
            for d in range(3):
                total += xr[j, d, at].astype(F32)
            return total

        zs[j] = rows_of(1 - zh).astype(BF)
        z_copy(j).start()
        keep[j] = rows_of(zh)

    def over_z(j):
        z_copy(j).wait_recv()
        total = (keep[j] + zr[j].astype(F32)).reshape(4, 32, 256)
        for p in (0, 1):
            out[:, p, :, j * 128 : (j + 1) * 128] = total[..., p * 128 : (p + 1) * 128]

    def fwd(j):
        return send(mir.at[0, j], mir.at[1, j], s_fwd.at[j], r_fwd.at[j], partner)

    def arrive(j):
        mlocal[j].wait()
        fwd(j).start()

    for j in range(CHUNKS):
        arrive(j)
        fwd(j).wait_recv()
        product(j)
        if j >= 1:
            over_x(j - 1)
        if j >= 2:
            over_z(j - 2)
    over_x(CHUNKS - 1)
    over_z(CHUNKS - 2)
    over_z(CHUNKS - 1)

    for cp in [*f1, *f2, f3, *swap]:
        cp.wait_send()

    @pl.when(far_mirror)
    def _():
        for cp in mcopy:
            cp.wait_send()

    for j in range(CHUNKS):
        fwd(j).wait_send()
        for d in range(3):
            x_copy(j, d).wait_send()
        z_copy(j).wait_send()


def on_device(perambulator, meson_field, op_momentum, op_gamma):
    tau = perambulator.reshape(2, 8, 2, 32, 512)
    tab = jnp.asarray(spin_table())
    smem = pl.BlockSpec(memory_space=pltpu.SMEM)
    vmem = pl.BlockSpec(memory_space=pltpu.VMEM)
    dma = pltpu.SemaphoreType.DMA
    loops = pl.pallas_call(
        kernel,
        out_shape=jax.ShapeDtypeStruct((4, 2, 32, 512), F32),
        in_specs=[smem, smem, smem, pl.BlockSpec(memory_space=pl.ANY), vmem],
        out_specs=vmem,
        scratch_shapes=[
            pltpu.VMEM((4, 2, 16, 8, 128), BF),
            pltpu.VMEM((4, 2, 16, 8, 128), BF),
            pltpu.VMEM((2, 4, 8, 32, 128), BF),
            pltpu.VMEM((2, 4, 8, 32, 128), BF),
            pltpu.VMEM((2, CHUNKS, 2, 2, 2, 32, 512), BF),
            pltpu.VMEM((2, 2, 4, 2, 4, 32, 512), BF),
            pltpu.VMEM((2, 2, 512, 256), BF),
            pltpu.VMEM((CHUNKS, 256, 256), F32),
            pltpu.VMEM((CHUNKS, 3, 256, 256), BF),
            pltpu.VMEM((CHUNKS, 3, 256, 256), BF),
            pltpu.VMEM((CHUNKS, 128, 256), F32),
            pltpu.VMEM((CHUNKS, 128, 256), BF),
            pltpu.VMEM((CHUNKS, 128, 256), BF),
            dma((2, 4)), dma((2, 4)), dma((2, 4)), dma((3,)), dma((3,)), dma((3,)), dma((3,)), dma(()), dma(()),
            dma((CHUNKS,)), dma((CHUNKS,)), dma((CHUNKS,)), dma((CHUNKS,)),
            dma((CHUNKS, 3)), dma((CHUNKS, 3)), dma((CHUNKS,)), dma((CHUNKS,)),
        ],
        compiler_params=pltpu.CompilerParams(
            collective_id=0, has_side_effects=True, vmem_limit_bytes=48 * 1024 * 1024
        ),
        name="loops",
    )(op_gamma, op_momentum, tab, tau, meson_field)
    return jnp.transpose(loops, (2, 0, 1, 3)).reshape(32, 1, 4, 2, 512)


def solution(mesh):
    return jax.shard_map(
        on_device,
        mesh=mesh,
        in_specs=(P("src", "snk"), P("snk", None, None, "src"), P(), P()),
        out_specs=P("snk", "src"),
        check_vma=False,
    )
```

time: 299 us -> 103 us (0.34)
  waiting for transfers between devices: 189 us -> 0 us
  Pallas kernels: 0 us -> 98.2 us
  blocking collectives: 35.8 us -> 0 us
  starting transfers between devices: 21.5 us -> 0 us
  matrix products: 16.2 us -> 0 us
  local copies, waits for them, and re-layouts: 20.8 us -> 4.65 us
  between operations: 13.6 us -> 0.01 us
    reduce_scatter x2 -> x0, waiting for transfers between devices: 146 us -> none  [the longest x1 127 us: summed_rows(): return lax.psum_scatter(parts, chips, scatter_dimension=0, tiled=True)[0]]
    pallas_call x0 -> x1, Pallas kernels: none -> 98.2 us  [on_device(): pl.pallas_call(kernel, out_shape=jax.ShapeDtypeStruct((4, 2, 32, 512), F3...]
    all_to_all x3 -> x0, waiting for transfers between devices: 43 us -> none  [the longest x1 26.8 us: on_device(): lax.all_to_all(by_sink, 'src', split_axis=1, concat_axis=0, tiled=True)]
    all_to_all x1 -> x0, blocking collectives: 35.8 us -> none  [on_device(): lax.all_to_all(pieces, SNK, split_axis=3, concat_axis=1, tiled=True)]
    all_to_all x3 -> x0, starting transfers between devices: 21.5 us -> none  [the longest x1 9.17 us: copy_for_each(): return lax.all_to_all(copies, axis, split_axis=0, concat_axis=0, tiled=True)]
    dot_general x6 -> x0, matrix products: 16.2 us -> none  [the longest x1 5.44 us: on_device(): jnp.einsum('bkratx,bkxy->bkraty', turned, mixing, preferred_element_type=...]
    convert_element_type x2 -> x0, local copies, waits for them, and re-layouts: 7.49 us -> none  [the longest x1 7.49 us: on_device(): turned = jnp.einsum('abirsm,kisjt->bkratjm', forward, gamma_pair, preferr...]
    transpose x1 -> x0, local copies, waits for them, and re-layouts: 4.32 us -> none  [summed_rows(): parts = parts.reshape(*sizes, *inside).swapaxes(0, 1).reshape(-1, *inside)]
  transfers between devices with their start and end apart: 5 -> 0, of which waited for: 5 -> 0; matrix products, arithmetic and copies ran while one was open for 7% -> 0% of each run, Pallas kernels for 0% -> 0%
where the time goes in v1:
time: 103 us
  Pallas kernels  98.2 us (95%)
  local copies, waits for them, and re-layouts  4.65 us (5%)
    pallas_call x1, Pallas kernels, on_device(): pl.pallas_call(kernel, out_shape=jax.ShapeDtypeStruct((4, 2, 32, 512), F3...  98.2 us
    unnamed x10, local copies, waits for them, and re-layouts  3.46 us

profile of v1, /device:TPU:1, one launch (start us, length us, event | category | flops | bytes accessed | tf_op | source)
XLA Modules:
  0.0 102.8 jit_solution(545944878521544251)
XLA Ops:
  0.0 0.0 copy-start.2
  0.0 0.0 copy-start.3
  0.0 0.7 copy-done.2
  0.7 0.0 copy-done.3
  0.7 0.0 copy-start
  0.7 1.2 %copy-done = bf16[1,1,2,512,512]{4,3,2,1,0:T(8,128)(2,1)S(1)} copy-done((bf16[1,1,2,512,512]{4,3,2,1,0:T(8,128)(2,1)S(1)}, bf16[1,1,2,512,512]{4,3,2,1,0:T(8,128)(2,1)}, u32[]{:S(2)}) %copy-start) | copy-done | bytes 1048600
  1.9 0.0 copy-start.1
  1.9 0.9 copy-done.1
  2.8 0.0 copy-start.4
  2.8 0.7 copy-done.4
  3.5 98.2 %loops.1 = f32[4,2,32,512]{3,2,1,0:T(8,128)S(1)} custom-call(s32[4]{0:T(128)S(1)} %copy-done.3, s32[4]{0:T(128)S(1)} %copy-done.4, s32[192]{0:T(256)S(1)} %copy-done.2, bf16[2,8,2,32,512]{4,3,2,1,0:T(8,128)(2,1)S(1)} %bitcast.5, bf16[1,27,2,8,128]{4,3,2,1,0:T(8,128)(2,1)S(1)} %copy-done.1), custom_call_target="tpu_custom_call" | custom-call | tf_op jit(solution)/shard_map/loops/pallas_call | solution.py:262
  101.6 1.2 %copy.6 = f32[32,1,4,2,512]{4,3,2,1,0:T(2,128)} copy(f32[32,1,4,2,512]{4,0,3,2,1:T(8,128)S(1)} %bitcast.4) | data formatting | bytes 1048576 | tf_op jit(solution)/shard_map/reshape | solution.py:290
Async XLA Ops:
  0.0 0.7 copy-start.2
  0.0 0.7 copy-start.3
  0.7 1.2 %copy-start = (bf16[1,1,2,512,512]{4,3,2,1,0:T(8,128)(2,1)S(1)}, bf16[1,1,2,512,512]{4,3,2,1,0:T(8,128)(2,1)}, u32[]{:S(2)}) copy-start(bf16[1,1,2,512,512]{4,3,2,1,0:T(8,128)(2,1)} %param.5) | copy-start | bytes 3145732
  1.9 0.9 copy-start.1
  2.8 0.7 copy-start.4

commit v2 on v1

--- a/solution.py
+++ b/solution.py
@@ -9,6 +9,7 @@
 MESH = pl.DeviceIdType.MESH
 NX, NY, NZ = 4, 4, 8
 CHUNKS = 4
+LONG = (1, 3)
 BF, F32 = jnp.bfloat16, jnp.float32
 
 
@@ -43,31 +44,79 @@
     return (y * 4 + z % 4, x * 4 + (z // 4) * 2 + c)
 
 
-def kernel(gam, mom, tab, tau, mes, out, field, field_b, half, half_b, mir, front, turn, mine, xs, xr, keep, zs, zr,
+def goes_around(z, c):
+    return (z == 2) | (z == 5) | ((z == 3) & (c == 1)) | ((z == 4) & (c == 0))
+
+
+def kernel(gam_in, mom_in, tab_in, tau, mes_in, out, gam, mom, tab, mes, field, field_b, half, half_b, mir, front, turn, mine, xs, xr, keep, zs, zr, ybuf, wbuf, turned,
            s_loc, s_half, r_half, s_f1, r_f1, s_f2, r_f2, s_f3, r_f3, s_mir, r_mir, s_fwd, r_fwd,
-           s_x, r_x, s_z, r_z):
+           s_x, r_x, s_z, r_z, s_y, r_y, s_w, r_w, s_t, r_t):
     src, snk = lax.axis_index("src"), lax.axis_index("snk")
     x, y, zh, zl, c = snk // 4, src // 4, (snk // 2) % 2, src % 4, snk % 2
     z = zh * 4 + zl
     l1, l0 = zl // 2, zl % 2
     other = 1 - c
     partner = place(x, y, z, other)
-    mirror = place(y, x, l1 * 4 + zh * 2 + c, l0)
-    own_mirror = (mirror[0] == src) & (mirror[1] == snk)
-    far_mirror = jnp.logical_not(own_mirror)
+    zm, cm = l1 * 4 + zh * 2 + c, l0
+    across = place(y, x, z, c)
+    around, around_in = goes_around(z, c), goes_around(zm, cm)
+    end = (z == 0) | (z == 7)
+    end_two = ((z == 7) & (c == 0)) | ((z == 0) & (c == 1))
+    w_slot = jnp.where((z == 2) | (z == 5), 0, 1)
+    up = z == 7
+    w_ends = (
+        (end, place(x, y, jnp.where(up, 2, 5), c), place(x, y, jnp.where(up, 4 + c, 2 + c), jnp.where(up, 0, 1))),
+        (end_two, place(x, y, jnp.where(up, 4, 3), c), place(x, y, jnp.where(up, 2, 5), jnp.where(up, 0, 1))),
+    )
+    diag, off = x == y, x != y
+    stays = (z == zm) & (c == cm)
+    moves = jnp.logical_not(stays)
+    z_mirror = place(x, y, zm, cm)
+    far_relay = place(x, y, 7 * (1 - z % 2), c)
+    far_relay_in = place(x, y, 7 * (1 - zm % 2), cm)
+
+    def behind(i):
+        return (y + 4 - i) % 4
+
+    def relays(i):
+        return x != behind(i)
+
     zl_peers = [place(x, y, zh * 4 + (zl + d) % 4, c) for d in (1, 2, 3)]
     y_peers = [place(x, (y + d) % 4, z, c) for d in (1, 2, 3)]
     x_peers = [place((x + d) % 4, y, z, c) for d in (1, 2, 3)]
     z_peer = place(x, y, (z + 4) % 8, c)
 
+    pltpu.make_async_copy(mes_in, mes, s_loc.at[1, 3]).start()
+    pltpu.make_async_copy(gam_in, gam, s_loc.at[0, 0]).start()
+    pltpu.make_async_copy(mom_in, mom, s_loc.at[0, 1]).start()
+    pltpu.make_async_copy(tab_in, tab, s_loc.at[0, 2]).start()
     bar = pltpu.get_barrier_semaphore()
     for dev in [partner, z_peer, *zl_peers, *y_peers, *x_peers]:
         pl.semaphore_signal(bar, inc=1, device_id=dev, device_id_type=MESH)
 
-    @pl.when(far_mirror)
-    def _():
-        pl.semaphore_signal(bar, inc=1, device_id=mirror, device_id_type=MESH)
-
+    def greet(cond, *devs):
+        @pl.when(cond)
+        def _():
+            for dev in devs:
+                pl.semaphore_signal(bar, inc=1, device_id=dev, device_id_type=MESH)
+
+        return jnp.where(cond, len(devs), 0)
+
+    peers = 11
+    peers += greet(off, across)
+    for i in (1, 2, 3):
+        peers += greet(relays(i), place(behind(i), x, z, c))
+        peers += greet(off, place(y, (x + i) % 4, z, c))
+    peers += greet(moves, z_mirror)
+    peers += greet(around, far_relay)
+    peers += greet(around_in, far_relay_in)
+    for cond, dev_from, dev_to in w_ends:
+        peers += greet(cond, dev_from, dev_to)
+
+    pltpu.make_async_copy(mes_in, mes, s_loc.at[1, 3]).wait()
+    pltpu.make_async_copy(gam_in, gam, s_loc.at[0, 0]).wait()
+    pltpu.make_async_copy(mom_in, mom, s_loc.at[0, 1]).wait()
+    pltpu.make_async_copy(tab_in, tab, s_loc.at[0, 2]).wait()
     for k in range(4):
         field[k, :, src] = mes[0, mom[k]]
     local = [
@@ -80,7 +129,7 @@
     for cp in local:
         cp.start()
 
-    pl.semaphore_wait(bar, jnp.where(far_mirror, 12, 11))
+    pl.semaphore_wait(bar, peers)
 
     def send(a, b, ss, rs, dev):
         return pltpu.make_async_remote_copy(
@@ -106,29 +155,109 @@
     ]
     for cp in swap:
         cp.start()
-    mcopy = [
-        send(tau.at[:, pl.ds(2 * j, 2)], mir.at[0, j], s_mir.at[j], r_mir.at[j], mirror)
-        for j in range(CHUNKS)
-    ]
-    mlocal = [
-        pltpu.make_async_copy(tau.at[:, pl.ds(2 * j, 2)], mir.at[0, j], r_mir.at[j])
-        for j in range(CHUNKS)
-    ]
-
-    @pl.when(far_mirror)
-    def _():
-        for cp in mcopy:
-            cp.start()
-
-    @pl.when(own_mirror)
-    def _():
-        for cp in mlocal:
-            cp.start()
+    def rows(j, i):
+        return tau.at[:, 2 * j + i // 2, i % 2]
+
+    def landed(ref, sem):
+        pltpu.make_async_copy(ref, ref, sem).wait()
+
+    def to_relay(j, i):
+        dev = place(x, (y + i) % 4, z, c)
+        return send(rows(j, i), ybuf.at[j, i - 1], s_mir.at[j, i], r_y.at[j, i - 1], dev)
+
+    def step_across(j, i, final):
+        dst, sem = (mir.at[0, j, i], r_mir.at[j, i]) if final else (turned.at[j, i], r_t.at[j, i])
+        if i == 0:
+            return send(rows(j, 0), dst, s_mir.at[j, 0], sem, across)
+        dev = place(behind(i), x, z, c)
+        return send(ybuf.at[j, i - 1], dst, s_y.at[j, i - 1], sem, dev)
+
+    def along_z(j, i, ref):
+        return send(ref, mir.at[0, j, i], s_t.at[j, i], r_mir.at[j, i], z_mirror)
+
+    def to_far_relay(j, i, ref):
+        return send(ref, wbuf.at[j, i // 2, w_slot], s_t.at[j, i], r_w.at[j, i // 2, w_slot], far_relay)
+
+    def from_far_relay(j, i, e):
+        k = i // 2
+        return send(wbuf.at[j, k, e], mir.at[0, j, i], s_w.at[j, k, e], r_mir.at[j, i], w_ends[e][2])
+
+    def local_piece(j, i):
+        return pltpu.make_async_copy(rows(j, i), mir.at[0, j, i], r_mir.at[j, i])
+
+    def start_z(j, i, ref):
+        if i in LONG:
+
+            @pl.when(around)
+            def _():
+                to_far_relay(j, i, ref).start()
+
+            @pl.when(jnp.logical_not(around))
+            def _():
+                along_z(j, i, ref).start()
+        else:
+            along_z(j, i, ref).start()
+
+    def stage_a(j):
+        @pl.when(off)
+        def _():
+            for i in (1, 3, 2):
+                to_relay(j, i).start()
+
+        @pl.when(diag & moves)
+        def _():
+            for i in (1, 3, 0, 2):
+                start_z(j, i, rows(j, i))
+
+        @pl.when(diag & stays)
+        def _():
+            for i in range(4):
+                local_piece(j, i).start()
+
+    def stage_b(j):
+        def go(i):
+            @pl.when(stays)
+            def _():
+                step_across(j, i, True).start()
+
+            @pl.when(moves)
+            def _():
+                step_across(j, i, False).start()
+
+        @pl.when(off)
+        def _():
+            go(0)
+
+        for i in (1, 3, 2):
+
+            @pl.when(relays(i))
+            def _():
+                landed(ybuf.at[j, i - 1], r_y.at[j, i - 1])
+                go(i)
+
+    def stage_c(j):
+        @pl.when(off & moves)
+        def _():
+            for i in (0, 1, 3, 2):
+                landed(turned.at[j, i], r_t.at[j, i])
+                start_z(j, i, turned.at[j, i])
+
+    def stage_w(j):
+        for e in range(2):
+
+            @pl.when(w_ends[e][0])
+            def _():
+                for i in LONG:
+                    landed(wbuf.at[j, i // 2, e], r_w.at[j, i // 2, e])
+                    from_far_relay(j, i, e).start()
+
+    for j in range(CHUNKS):
+        stage_a(j)
 
     for d in range(3):
         send(field.at[:, :, src], field.at[:, :, src], s_f1.at[d], r_f1.at[d], zl_peers[d]).wait_recv()
-    rows = field.at[:, :, pl.ds(4 * y, 4)]
-    f2 = [send(rows, rows, s_f2.at[d], r_f2.at[d], y_peers[d]) for d in range(3)]
+    mine_y = field.at[:, :, pl.ds(4 * y, 4)]
+    f2 = [send(mine_y, mine_y, s_f2.at[d], r_f2.at[d], y_peers[d]) for d in range(3)]
     for cp in f2:
         cp.start()
     for cp in f2:
@@ -163,12 +292,17 @@
 
         lax.fori_loop(0, 4, for_op, 0)
 
+    stage_b(0)
     make_front(0, field, half)
+    stage_b(1)
+    stage_c(0)
     f3.wait_recv()
     for cp in swap:
         cp.wait_recv()
     make_front(1, field_b, half_b)
-
+    stage_b(2)
+    stage_c(1)
+    stage_w(0)
     def x_copy(j, d):
         return send(xs.at[j, d], xr.at[j, d], s_x.at[j, d], r_x.at[j, d], x_peers[d])
 
@@ -177,8 +311,8 @@
 
     def product(j):
         for b in (0, 1):
-            re = mir[b, j, 0].reshape(128, 512)
-            im = mir[b, j, 1].reshape(128, 512)
+            re = mir[b, j, :, 0].reshape(128, 512)
+            im = mir[b, j, :, 1].reshape(128, 512)
             if j >= 2:
                 re, im = -re, -im
             turn[b, 0] = jnp.concatenate([re, -im], axis=0).T
@@ -219,17 +353,26 @@
         for p in (0, 1):
             out[:, p, :, j * 128 : (j + 1) * 128] = total[..., p * 128 : (p + 1) * 128]
 
-    def fwd(j):
-        return send(mir.at[0, j], mir.at[1, j], s_fwd.at[j], r_fwd.at[j], partner)
+    def fwd(j, q):
+        return send(mir.at[0, j, q], mir.at[1, j, q], s_fwd.at[j, q], r_fwd.at[j, q], partner)
 
     def arrive(j):
-        mlocal[j].wait()
-        fwd(j).start()
+        for q in (0, 2, 1, 3):
+            local_piece(j, q).wait()
+            fwd(j, q).start()
 
     for j in range(CHUNKS):
         arrive(j)
-        fwd(j).wait_recv()
+        for q in (0, 2, 1, 3):
+            fwd(j, q).wait_recv()
         product(j)
+        if j + 1 < CHUNKS:
+            stage_w(j + 1)
+        if j == 0:
+            stage_b(3)
+            stage_c(2)
+        if j == 1:
+            stage_c(3)
         if j >= 1:
             over_x(j - 1)
         if j >= 2:
@@ -241,13 +384,34 @@
     for cp in [*f1, *f2, f3, *swap]:
         cp.wait_send()
 
-    @pl.when(far_mirror)
-    def _():
-        for cp in mcopy:
-            cp.wait_send()
-
     for j in range(CHUNKS):
-        fwd(j).wait_send()
+
+        @pl.when(off)
+        def _():
+            step_across(j, 0, False).wait_send()
+            for i in (1, 2, 3):
+                to_relay(j, i).wait_send()
+
+        @pl.when(moves)
+        def _():
+            for i in range(4):
+                along_z(j, i, turned.at[j, i]).wait_send()
+
+        for i in (1, 2, 3):
+
+            @pl.when(relays(i))
+            def _():
+                step_across(j, i, False).wait_send()
+
+        for e in range(2):
+
+            @pl.when(w_ends[e][0])
+            def _():
+                for i in LONG:
+                    from_far_relay(j, i, e).wait_send()
+
+        for q in range(4):
+            fwd(j, q).wait_send()
         for d in range(3):
             x_copy(j, d).wait_send()
         z_copy(j).wait_send()
@@ -256,20 +420,23 @@
 def on_device(perambulator, meson_field, op_momentum, op_gamma):
     tau = perambulator.reshape(2, 8, 2, 32, 512)
     tab = jnp.asarray(spin_table())
-    smem = pl.BlockSpec(memory_space=pltpu.SMEM)
     vmem = pl.BlockSpec(memory_space=pltpu.VMEM)
     dma = pltpu.SemaphoreType.DMA
     loops = pl.pallas_call(
         kernel,
         out_shape=jax.ShapeDtypeStruct((4, 2, 32, 512), F32),
-        in_specs=[smem, smem, smem, pl.BlockSpec(memory_space=pl.ANY), vmem],
+        in_specs=[pl.BlockSpec(memory_space=pl.ANY)] * 5,
         out_specs=vmem,
         scratch_shapes=[
+            pltpu.SMEM((4,), jnp.int32),
+            pltpu.SMEM((4,), jnp.int32),
+            pltpu.SMEM((192,), jnp.int32),
+            pltpu.VMEM((1, 27, 2, 8, 128), BF),
             pltpu.VMEM((4, 2, 16, 8, 128), BF),
             pltpu.VMEM((4, 2, 16, 8, 128), BF),
             pltpu.VMEM((2, 4, 8, 32, 128), BF),
             pltpu.VMEM((2, 4, 8, 32, 128), BF),
-            pltpu.VMEM((2, CHUNKS, 2, 2, 2, 32, 512), BF),
+            pltpu.VMEM((2, CHUNKS, 4, 2, 32, 512), BF),
             pltpu.VMEM((2, 2, 4, 2, 4, 32, 512), BF),
             pltpu.VMEM((2, 2, 512, 256), BF),
             pltpu.VMEM((CHUNKS, 256, 256), F32),
@@ -278,12 +445,16 @@
             pltpu.VMEM((CHUNKS, 128, 256), F32),
             pltpu.VMEM((CHUNKS, 128, 256), BF),
             pltpu.VMEM((CHUNKS, 128, 256), BF),
+            pltpu.VMEM((CHUNKS, 3, 2, 32, 512), BF),
+            pltpu.VMEM((CHUNKS, 2, 2, 2, 32, 512), BF),
+            pltpu.VMEM((CHUNKS, 4, 2, 32, 512), BF),
             dma((2, 4)), dma((2, 4)), dma((2, 4)), dma((3,)), dma((3,)), dma((3,)), dma((3,)), dma(()), dma(()),
-            dma((CHUNKS,)), dma((CHUNKS,)), dma((CHUNKS,)), dma((CHUNKS,)),
+            dma((CHUNKS, 4)), dma((CHUNKS, 4)), dma((CHUNKS, 4)), dma((CHUNKS, 4)),
             dma((CHUNKS, 3)), dma((CHUNKS, 3)), dma((CHUNKS,)), dma((CHUNKS,)),
+            dma((CHUNKS, 3)), dma((CHUNKS, 3)), dma((CHUNKS, 2, 2)), dma((CHUNKS, 2, 2)), dma((CHUNKS, 4)), dma((CHUNKS, 4)),
         ],
         compiler_params=pltpu.CompilerParams(
-            collective_id=0, has_side_effects=True, vmem_limit_bytes=48 * 1024 * 1024
+            collective_id=0, has_side_effects=True, vmem_limit_bytes=67_000_000
         ),
         name="loops",
     )(op_gamma, op_momentum, tab, tau, meson_field)

time: 103 us -> 91.7 us (0.89)
  Pallas kernels: 98.2 us -> 89.4 us
  local copies, waits for them, and re-layouts: 4.65 us -> 2.24 us
    pallas_call x1, Pallas kernels: 98.2 us -> 89.4 us  [on_device(): pl.pallas_call(kernel, out_shape=jax.ShapeDtypeStruct((4, 2, 32, 512), F3...]
    unnamed x10 -> x0, local copies, waits for them, and re-layouts: 3.46 us -> none
    reshape x1, local copies, waits for them, and re-layouts: 1.2 us -> 2.24 us  [on_device(): return jnp.transpose(loops, (2, 0, 1, 3)).reshape(32, 1, 4, 2, 512)]
where the time goes in v2:
time: 91.7 us; the launch traced here: 91.6 us
  Pallas kernels  89.4 us (97%)
  local copies, waits for them, and re-layouts  2.24 us (2%)
    pallas_call x1, Pallas kernels, on_device(): pl.pallas_call(kernel, out_shape=jax.ShapeDtypeStruct((4, 2, 32, 512), F3...  89.4 us
    reshape x1, local copies, waits for them, and re-layouts, on_device(): return jnp.transpose(loops, (2, 0, 1, 3)).reshape(32, 1, 4, 2, 512)  2.24 us

profile of v2, /device:TPU:1, one launch (start us, length us, event | category | flops | bytes accessed | tf_op | source)
XLA Modules:
  0.0 91.6 jit_solution(7797179305218672158)
XLA Ops:
  0.0 89.4 %loops.1 = f32[4,2,32,512]{3,2,1,0:T(8,128)} custom-call(s32[4]{0:T(128)} %gam_in.1, s32[4]{0:T(128)} %mom_in.1, s32[192]{0:T(256)} %constant.2.clone.tab_in, bf16[2,8,2,32,512]{4,3,2,1,0:T(8,128)(2,1)} %bitcast.5, bf16[1,27,2,8,128]{4,3,2,1,0:T(8,128)(2,1)} %mes_in.1), custom_call_target="tpu_custom_call" | custom-call | tf_op jit(solution)/shard_map/loops/pallas_call | solution.py:425
  89.4 2.2 %copy.6 = f32[32,1,4,2,512]{4,3,2,1,0:T(2,128)} copy(f32[32,1,4,2,512]{4,0,3,2,1:T(8,128)} %bitcast.4) | data formatting | bytes 1048576 | tf_op jit(solution)/shard_map/reshape | solution.py:461

commit v3 on v2

--- a/solution.py
+++ b/solution.py
@@ -251,8 +251,8 @@
                     landed(wbuf.at[j, i // 2, e], r_w.at[j, i // 2, e])
                     from_far_relay(j, i, e).start()
 
-    for j in range(CHUNKS):
-        stage_a(j)
+    stage_a(0)
+    stage_a(1)
 
     for d in range(3):
         send(field.at[:, :, src], field.at[:, :, src], s_f1.at[d], r_f1.at[d], zl_peers[d]).wait_recv()
@@ -293,15 +293,17 @@
         lax.fori_loop(0, 4, for_op, 0)
 
     stage_b(0)
+    stage_a(2)
     make_front(0, field, half)
+    stage_c(0)
     stage_b(1)
-    stage_c(0)
+    stage_a(3)
     f3.wait_recv()
     for cp in swap:
         cp.wait_recv()
     make_front(1, field_b, half_b)
+    stage_c(1)
     stage_b(2)
-    stage_c(1)
     stage_w(0)
     def x_copy(j, d):
         return send(xs.at[j, d], xr.at[j, d], s_x.at[j, d], r_x.at[j, d], x_peers[d])
@@ -363,16 +365,16 @@
 
     for j in range(CHUNKS):
         arrive(j)
+        if j == 0:
+            stage_b(3)
+            stage_c(2)
+        if j == 1:
+            stage_c(3)
         for q in (0, 2, 1, 3):
             fwd(j, q).wait_recv()
         product(j)
         if j + 1 < CHUNKS:
             stage_w(j + 1)
-        if j == 0:
-            stage_b(3)
-            stage_c(2)
-        if j == 1:
-            stage_c(3)
         if j >= 1:
             over_x(j - 1)
         if j >= 2:
@@ -454,7 +456,7 @@
             dma((CHUNKS, 3)), dma((CHUNKS, 3)), dma((CHUNKS, 2, 2)), dma((CHUNKS, 2, 2)), dma((CHUNKS, 4)), dma((CHUNKS, 4)),
         ],
         compiler_params=pltpu.CompilerParams(
-            collective_id=0, has_side_effects=True, vmem_limit_bytes=67_000_000
+            collective_id=0, has_side_effects=True, vmem_limit_bytes=66_200_000
         ),
         name="loops",
     )(op_gamma, op_momentum, tab, tau, meson_field)

time: 91.7 us -> 87 us (0.949)
  Pallas kernels: 89.4 us -> 84.6 us
    pallas_call x1, Pallas kernels: 89.4 us -> 84.6 us  [on_device(): pl.pallas_call(kernel, out_shape=jax.ShapeDtypeStruct((4, 2, 32, 512), F3...]
where the time goes in v3:
time: 87 us; the launch traced here: 86.9 us
  Pallas kernels  84.6 us (97%)
  local copies, waits for them, and re-layouts  2.24 us (3%)
    pallas_call x1, Pallas kernels, on_device(): pl.pallas_call(kernel, out_shape=jax.ShapeDtypeStruct((4, 2, 32, 512), F3...  84.6 us
    reshape x1, local copies, waits for them, and re-layouts, on_device(): return jnp.transpose(loops, (2, 0, 1, 3)).reshape(32, 1, 4, 2, 512)  2.24 us

profile of v3, /device:TPU:1, one launch (start us, length us, event | category | flops | bytes accessed | tf_op | source)
XLA Modules:
  0.0 86.9 jit_solution(999667428696379527)
XLA Ops:
  0.0 84.6 %loops.1 = f32[4,2,32,512]{3,2,1,0:T(8,128)} custom-call(s32[4]{0:T(128)} %gam_in.1, s32[4]{0:T(128)} %mom_in.1, s32[192]{0:T(256)} %constant.2.clone.tab_in, bf16[2,8,2,32,512]{4,3,2,1,0:T(8,128)(2,1)} %bitcast.5, bf16[1,27,2,8,128]{4,3,2,1,0:T(8,128)(2,1)} %mes_in.1), custom_call_target="tpu_custom_call" | custom-call | tf_op jit(solution)/shard_map/loops/pallas_call | solution.py:427
  84.7 2.2 %copy.6 = f32[32,1,4,2,512]{4,3,2,1,0:T(2,128)} copy(f32[32,1,4,2,512]{4,0,3,2,1:T(8,128)} %bitcast.4) | data formatting | bytes 1048576 | tf_op jit(solution)/shard_map/reshape | solution.py:463

commit v4 on v3

--- a/solution.py
+++ b/solution.py
@@ -254,18 +254,6 @@
     stage_a(0)
     stage_a(1)
 
-    for d in range(3):
-        send(field.at[:, :, src], field.at[:, :, src], s_f1.at[d], r_f1.at[d], zl_peers[d]).wait_recv()
-    mine_y = field.at[:, :, pl.ds(4 * y, 4)]
-    f2 = [send(mine_y, mine_y, s_f2.at[d], r_f2.at[d], y_peers[d]) for d in range(3)]
-    for cp in f2:
-        cp.start()
-    for cp in f2:
-        cp.wait_recv()
-    f3 = send(field, field_b, s_f3, r_f3, partner)
-    f3.start()
-    for cp in local:
-        cp.wait()
 
     def make_front(b, field, half):
         def for_op(k, carry):
@@ -292,10 +280,22 @@
 
         lax.fori_loop(0, 4, for_op, 0)
 
+    for d in range(3):
+        send(field.at[:, :, src], field.at[:, :, src], s_f1.at[d], r_f1.at[d], zl_peers[d]).wait_recv()
+    mine_y = field.at[:, :, pl.ds(4 * y, 4)]
+    f2 = [send(mine_y, mine_y, s_f2.at[d], r_f2.at[d], y_peers[d]) for d in range(3)]
+    for cp in f2:
+        cp.start()
     stage_b(0)
     stage_a(2)
+    for cp in f2:
+        cp.wait_recv()
+    f3 = send(field, field_b, s_f3, r_f3, partner)
+    f3.start()
+    stage_c(0)
+    for cp in local:
+        cp.wait()
     make_front(0, field, half)
-    stage_c(0)
     stage_b(1)
     stage_a(3)
     f3.wait_recv()

time: 87 us -> 86.8 us (level)
  no operation moved by 1% of the time
where the time goes in v4:
time: 86.8 us; the launch traced here: 86.7 us
  Pallas kernels  84.4 us (97%)
  local copies, waits for them, and re-layouts  2.24 us (3%)
    pallas_call x1, Pallas kernels, on_device(): pl.pallas_call(kernel, out_shape=jax.ShapeDtypeStruct((4, 2, 32, 512), F3...  84.4 us
    reshape x1, local copies, waits for them, and re-layouts, on_device(): return jnp.transpose(loops, (2, 0, 1, 3)).reshape(32, 1, 4, 2, 512)  2.24 us

profile of v4, /device:TPU:1, one launch (start us, length us, event | category | flops | bytes accessed | tf_op | source)
XLA Modules:
  0.0 86.7 jit_solution(2284787714438805513)
XLA Ops:
  0.0 84.4 %loops.1 = f32[4,2,32,512]{3,2,1,0:T(8,128)} custom-call(s32[4]{0:T(128)} %gam_in.1, s32[4]{0:T(128)} %mom_in.1, s32[192]{0:T(256)} %constant.2.clone.tab_in, bf16[2,8,2,32,512]{4,3,2,1,0:T(8,128)(2,1)} %bitcast.5, bf16[1,27,2,8,128]{4,3,2,1,0:T(8,128)(2,1)} %mes_in.1), custom_call_target="tpu_custom_call" | custom-call | tf_op jit(solution)/shard_map/loops/pallas_call | solution.py:427
  84.4 2.2 %copy.6 = f32[32,1,4,2,512]{4,3,2,1,0:T(2,128)} copy(f32[32,1,4,2,512]{4,0,3,2,1:T(8,128)} %bitcast.4) | data formatting | bytes 1048576 | tf_op jit(solution)/shard_map/reshape | solution.py:463
